TPU v7x, 32 devices: a whole 2x2x4 slice. The times are simulated.
32 devices in a mesh: row: 4 (over y, core), col: 8 (over z, x).
Axes of the slice: x: 2, y: 2, z: 4, core: 2. Of those that a mesh axis runs over, the one named last changes fastest.
Arguments:
- matrix: float32 [16, 4, 256, 8, 8, 256], P(None, 'row', None, None, 'col'), may hold values from -10 to 20, as said below
Outputs:
- factored: float32 [16, 4, 256, 8, 8, 256], P(None, 'row', None, None, 'col')
Inputs may be any that keep to these rules, and one draw needn't show every extreme that they name: matrix is symmetric, and its leading 2 * 256 rows and columns form a positive definite block.
All inputs are finite; a program needn't handle non-finite values.
Results may differ from a plain program's by a relative error of at most 0.0001.
Values sent between devices are 32-bit elements; how exact they have to be, the bound alone decides.
A program may use at most 192 MiB of HBM per device.

v0:
```python
import jax
import jax.numpy as jnp
from jax import lax
from jax.sharding import PartitionSpec as P

STEPS = 2


def broadcast(value, axis, source):
    kept = jnp.where(lax.axis_index(axis) == source, value, 0).astype(value.dtype)
    return lax.psum(kept, axis)


def local(matrix):
    block_rows, _, tile_edge, block_cols, _, _ = matrix.shape
    blocks = matrix.reshape(block_rows, tile_edge, block_cols, tile_edge)
    row_count = lax.axis_size("row")
    col_count = lax.axis_size("col")
    here_row = lax.axis_index("row")
    here_col = lax.axis_index("col")
    row_ids = jnp.arange(block_rows) * row_count + here_row
    col_ids = jnp.arange(block_cols) * col_count + here_col
    identity = jnp.eye(tile_edge, dtype=jnp.float32)

    def panels(blocks, section_at):
        diag_row = section_at // row_count
        diag_col = section_at // col_count
        diagonal = broadcast(blocks[diag_row, :, diag_col, :], "row", section_at % row_count)
        diag_factor = jnp.linalg.cholesky(diagonal)
        diag_inverse = jax.scipy.linalg.solve_triangular(diag_factor, identity, lower=True)
        factor_panel = jnp.einsum(
            "anb,cb->anc", blocks[:, :, diag_col, :], diag_inverse, precision=lax.Precision.HIGHEST
        )
        factor_panel = jnp.where(
            (row_ids > section_at)[:, None, None], factor_panel, jnp.zeros_like(factor_panel)
        )
        colvals = factor_panel + jnp.where(
            (row_ids == section_at)[:, None, None], diag_factor[None], jnp.zeros_like(factor_panel)
        )
        row_panel = broadcast(factor_panel, "col", section_at % col_count)
        source = broadcast(row_panel, "row", here_col % row_count)
        picked = jnp.arange(block_cols) * (col_count // row_count) + here_col // row_count
        col_panel = jnp.take(source, picked, axis=0)
        return (row_panel, col_panel, colvals)

    def trailing(blocks, pending, start, stop):
        if stop <= start:
            return blocks
        row_panel, col_panel, _ = pending
        update = jnp.einsum(
            "anb,cmb->ancm", row_panel, col_panel[start:stop], precision=lax.Precision.HIGHEST
        )
        return blocks.at[:, :, start:stop, :].add(-update)

    def finish(blocks, section_at, pending):
        diag_col = section_at // col_count
        on_col = here_col == section_at % col_count
        column = jnp.where(on_col, pending[2], blocks[:, :, diag_col, :])
        blocks = blocks.at[:, :, diag_col, :].set(column)
        zero_row = (row_ids == section_at)[:, None, None, None] & (col_ids > section_at)[
            None, None, :, None
        ]
        return jnp.where(zero_row, jnp.zeros_like(blocks), blocks)

    pending = panels(blocks, 0)
    for section_at in range(STEPS):
        if section_at + 1 < STEPS:
            next_col = (section_at + 1) // col_count
            blocks = trailing(blocks, pending, next_col, next_col + 1)
            blocks = finish(blocks, section_at, pending)
            upcoming = panels(blocks, section_at + 1)
            blocks = trailing(blocks, pending, 0, next_col)
            blocks = trailing(blocks, pending, next_col + 1, block_cols)
            pending = upcoming
        else:
            blocks = trailing(blocks, pending, 0, block_cols)
            blocks = finish(blocks, section_at, pending)
    return blocks.reshape(matrix.shape)


def solution(mesh):
    in_specs = (P(None, "row", None, None, "col", None),)
    out_specs = P(None, "row", None, None, "col", None)
    return jax.shard_map(local, mesh=mesh, in_specs=in_specs, out_specs=out_specs, check_vma=False)
```

profile of v0, /device:TPU:4, one launch (start us, length us, event | category | flops | bytes accessed | tf_op | source)
XLA Modules:
  0.0 983.2 jit_solution(6305789292915670719)
XLA Ops:
  6.5 78.2 %copy.2 = f32[16,1,256,8,1,256]{2,5,3,0,4,1:T(8,128)} copy(f32[16,1,256,8,1,256]{5,4,3,2,1,0:T(1,128)} %param.18) | data formatting | bytes 67108864 | tf_op args[0]
  86.5 32.1 %all-reduce.8.cloned.1.call-done = f32[256,256]{0,1:T(8,128)} async-done(((f32[256,256]{0,1:T(8,128)}), f32[256,256]{0,1:T(8,128)}) %all-reduce.8.cloned.1.call-update) | async-done | bytes 262160 | tf_op jit(solution)/shard_map/psum | solution.py:11
  120.7 11.7 %cholesky.130 = f32[128,128]{1,0:T(8,128)S(1)} custom-call(f32[128,128]{1,0:T(8,128)S(1)} %cholesky.194), custom_call_target="Cholesky" | custom-call | tf_op jit(solution)/shard_map/jit(cholesky)/cholesky | solution.py:29
  132.5 9.8 custom-call.13
  142.8 11.7 %cholesky.147 = f32[128,128]{1,0:T(8,128)S(1)} custom-call(f32[128,128]{1,0:T(8,128)S(1)} %convolution_subtract_fusion.3), custom_call_target="Cholesky" | custom-call | tf_op jit(solution)/shard_map/jit(cholesky)/cholesky | solution.py:29
  161.2 19.7 %custom-call.14 = f32[2,128,128]{1,2,0:T(8,128)S(1)} custom-call(f32[2,128,128]{2,1,0:T(8,128)S(1)} %get-tuple-element.90), custom_call_target="InvertDiagBlocksLowerTriangular" | custom-call | tf_op jit(solution)/shard_map/jit(_solve_triangular)/triangular_solve | solution.py:30
  181.8 9.2 bitcast_select_fusion
  191.1 157.9 %all-reduce.10.cloned.1.call-done = f32[16,256,256]{1,2,0:T(8,128)} async-done(((f32[16,256,256]{1,2,0:T(8,128)}), f32[16,256,256]{1,2,0:T(8,128)}) %all-reduce.10.cloned.1.call-update) | async-done | bytes 4194320 | tf_op jit(solution)/shard_map/psum | solution.py:11
  359.1 10.9 %copy.43 = f32[16,1,256,1,1,256]{2,5,0,4,3,1:T(8,128)} copy(f32[16,1,256,1,1,256]{5,4,3,2,1,0:T(1,128)} %slice.187) | data formatting | bytes 8388608
  370.3 66.2 %all-reduce.12.cloned.1.call-done = f32[16,256,256]{1,2,0:T(8,128)} async-done(((f32[16,256,256]{1,2,0:T(8,128)}), f32[16,256,256]{1,2,0:T(8,128)}) %all-reduce.12.cloned.1.call-update) | async-done | bytes 4194320 | tf_op jit(solution)/shard_map/psum | solution.py:11
  453.7 13.3 %broadcast_select_fusion = f32[16,256,8,256]{1,3,2,0:T(8,128)S(1)} fusion(f32[16,256,8,256]{1,3,2,0:T(8,128)} %bitcast_dynamic-update-slice_fusion.2, pred[16,8]{1,0:T(8,128)(4,1)S(1)} %broadcast_and_fusion), kind=kLoop, calls=%fused_computation.10 | loop fusion | flops 8388608 | bytes 67108992 | tf_op jit(solution)/shard_map/jit(_where)/select_n | solution.py:63
  467.1 11.7 %copy-done = f32[16,256,8,256]{1,3,2,0:T(8,128)} copy-done((f32[16,256,8,256]{1,3,2,0:T(8,128)}, f32[16,256,8,256]{1,3,2,0:T(8,128)S(1)}, u32[]{:S(2)}) %copy-start) | copy-done | bytes 33554456
  479.7 31.9 %all-reduce.14.cloned.1.call-done = f32[256,256]{0,1:T(8,128)} async-done(((f32[256,256]{0,1:T(8,128)}), f32[256,256]{0,1:T(8,128)}) %all-reduce.14.cloned.1.call-update) | async-done | bytes 262160 | tf_op jit(solution)/shard_map/psum | solution.py:11
  513.7 11.7 %cholesky.164 = f32[128,128]{1,0:T(8,128)S(1)} custom-call(f32[128,128]{1,0:T(8,128)S(1)} %cholesky.197), custom_call_target="Cholesky" | custom-call | tf_op jit(solution)/shard_map/jit(cholesky)/cholesky | solution.py:29
  525.5 9.8 custom-call.15
  535.8 11.7 %cholesky.181 = f32[128,128]{1,0:T(8,128)S(1)} custom-call(f32[128,128]{1,0:T(8,128)S(1)} %convolution_subtract_fusion.2), custom_call_target="Cholesky" | custom-call | tf_op jit(solution)/shard_map/jit(cholesky)/cholesky | solution.py:29
  554.2 19.7 %custom-call.16 = f32[2,128,128]{1,2,0:T(8,128)S(1)} custom-call(f32[2,128,128]{2,1,0:T(8,128)S(1)} %get-tuple-element.91), custom_call_target="InvertDiagBlocksLowerTriangular" | custom-call | tf_op jit(solution)/shard_map/jit(_solve_triangular)/triangular_solve | solution.py:30
  574.8 9.6 select_select_fusion
  584.7 157.7 %all-reduce.16.cloned.1.call-done = f32[16,256,256]{1,2,0:T(8,128)} async-done(((f32[16,256,256]{1,2,0:T(8,128)}), f32[16,256,256]{1,2,0:T(8,128)}) %all-reduce.16.cloned.1.call-update) | async-done | bytes 4194320 | tf_op jit(solution)/shard_map/psum | solution.py:11
  744.7 34.9 %fusion = f32[16,256,8,256]{1,3,2,0:T(8,128)} fusion(f32[16,256,8,256]{1,3,2,0:T(8,128)} %copy-done, f32[16,256,256]{1,2,0:T(8,128)} %all-reduce.10.cloned.1.call-done, f32[8,256,256]{1,2,0:T(8,128)S(1)} %broadcast_select_fusion.3), kind=kOutput, calls=%fused_computation.9 | convolution fusion | flops 22563258368 | bytes 64749568 | tf_op jit(solution)/shard_map/anb,cmb->ancm/dot_general | solution.py:50
  779.6 50.3 %all-reduce.18.cloned.1.call-done = f32[16,256,256]{1,2,0:T(8,128)} async-done(((f32[16,256,256]{1,2,0:T(8,128)}), f32[16,256,256]{1,2,0:T(8,128)}) %all-reduce.18.cloned.1.call-update) | async-done | bytes 4194320 | tf_op jit(solution)/shard_map/psum | solution.py:11
  832.8 37.0 %negate_add_fusion = f32[16,256,8,256]{1,3,2,0:T(8,128)} fusion(f32[16,256,8,256]{1,3,2,0:T(8,128)} %fusion, f32[16,256,256]{1,2,0:T(8,128)} %all-reduce.16.cloned.1.call-done, f32[8,256,256]{1,2,0:T(8,128)S(1)} %gather_fusion.1, pred[8]{0:T(512)(128)(4,1)S(1)} %compare_and_fusion), kind=kOutput, calls=%fused_computation.7 | convolution fusion | flops 25787105280 | bytes 73400328 | tf_op jit(solution)/shard_map/anb,cmb->ancm/dot_general | solution.py:50
  874.9 22.9 %select_bitcast_fusion = f32[16,1,256,8,1,256]{2,5,3,0,4,1:T(8,128)} fusion(f32[16,256,8,256]{1,3,2,0:T(8,128)} %fusion.3, pred[16,8]{1,0:T(8,128)(4,1)S(1)} %broadcast_and_fusion.1), kind=kLoop, calls=%fused_computation.6 | loop fusion | flops 8388608 | bytes 67108992 | tf_op jit(solution)/shard_map/reshape | solution.py:78
  897.8 78.2 %copy.23 = f32[16,1,256,8,1,256]{5,4,3,2,1,0:T(1,128)} copy(f32[16,1,256,8,1,256]{2,5,3,0,4,1:T(8,128)} %select_bitcast_fusion) | data formatting | bytes 67108864 | tf_op jit(solution)/shard_map/reshape | solution.py:78
  (89 shorter events, 66.6 us)
Async XLA Ops:
  6.5 112.1 %all-reduce.8.cloned.1.call-start = ((), (), s32[]{:S(2)}) async-start(), calls=%async_computation | async-start | bytes 524288 | tf_op jit(solution)/shard_map/psum | solution.py:11
  86.4 262.5 %all-reduce.10.cloned.1.call-start = ((), (), s32[]{:S(2)}) async-start(), calls=%async_computation.1 | async-start | bytes 8388608 | tf_op jit(solution)/shard_map/psum | solution.py:11
  191.0 245.5 %all-reduce.12.cloned.1.call-start = ((), (), s32[]{:S(2)}) async-start(), calls=%async_computation.2 | async-start | bytes 8388608 | tf_op jit(solution)/shard_map/psum | solution.py:11
  351.3 160.3 %all-reduce.14.cloned.1.call-start = ((), (), s32[]{:S(2)}) async-start(), calls=%async_computation.3 | async-start | bytes 524288 | tf_op jit(solution)/shard_map/psum | solution.py:11
  440.7 2.8 copy-start.1
  443.5 7.4 copy-start.2
  467.1 11.7 %copy-start = (f32[16,256,8,256]{1,3,2,0:T(8,128)}, f32[16,256,8,256]{1,3,2,0:T(8,128)S(1)}, u32[]{:S(2)}) copy-start(f32[16,256,8,256]{1,3,2,0:T(8,128)S(1)} %broadcast_select_fusion) | copy-start | bytes 100663296
  479.5 262.9 %all-reduce.16.cloned.1.call-start = ((), (), s32[]{:S(2)}) async-start(), calls=%async_computation.4 | async-start | bytes 8388608 | tf_op jit(solution)/shard_map/psum | solution.py:11
  584.4 245.5 %all-reduce.18.cloned.1.call-start = ((), (), s32[]{:S(2)}) async-start(), calls=%async_computation.5 | async-start | bytes 8388608 | tf_op jit(solution)/shard_map/psum | solution.py:11
  832.8 37.0 %copy-start.3 = (f32[16,256,256]{1,2,0:T(8,128)S(1)}, f32[16,256,256]{1,2,0:T(8,128)}, u32[]{:S(2)}) copy-start(f32[16,256,256]{1,2,0:T(8,128)} %get-tuple-element.133) | copy-start | bytes 12582916
Sparse Core Ops, SparseCore 0:
  86.6 32.0 all-reduce.7
  191.1 157.8 all-reduce.9
  351.4 85.0 all-reduce.11
  479.6 31.9 all-reduce.13
  584.5 157.8 all-reduce.15
  744.8 85.0 all-reduce.17
where the time goes:
time: 998 us; the launch traced here: 983 us
  waiting for transfers between devices  496 us (50%)
  local copies, waits for them, and re-layouts  205 us (21%)
  other arithmetic  163 us (16%)
  matrix products  101 us (10%)
  between operations  16.8 us (2%)
    psum x6, waiting for transfers between devices, broadcast(): return lax.psum(kept, axis)  496 us
    unnamed x10, local copies, waits for them, and re-layouts  102 us
    dot_general x3, matrix products, trailing(): jnp.einsum('anb,cmb->ancm', row_panel, col_panel[start:stop], precision=l...  79.3 us
    reshape x1, local copies, waits for them, and re-layouts, local(): return blocks.reshape(matrix.shape)  78.2 us
    another operation x13, other arithmetic, panels(): diag_factor = jnp.linalg.cholesky(diagonal)  68.6 us
    another operation x5, other arithmetic, panels(): jax.scipy.linalg.solve_triangular(diag_factor, identity, lower=True)  39.4 us
    reshape x1, other arithmetic, local(): return blocks.reshape(matrix.shape)  22.9 us
  transfers between devices with their start and end apart: 6, of which 6 were waited for; matrix products, arithmetic and copies ran while one was open for 6% of the time, Pallas kernels for 0%

commit v1 on v0

v1 whole, which is shorter than its diff:
```python
import functools

import jax
import jax.numpy as jnp
from jax import lax
from jax.experimental import pallas as pl
from jax.experimental.pallas import tpu as pltpu
from jax.sharding import PartitionSpec as P

LANES = 128
MESH_ID = pl.DeviceIdType.MESH
EXACT = lax.Precision.HIGHEST


def exchange(rows, cols, depth, m_ref, r_ref, c_ref, l_ref, ring_send, ring_recv,
             lead_send, lead_recv, wide_send, wide_recv, own_sem):
    row = lax.axis_index("row")
    col = lax.axis_index("col")
    half = cols // 2
    odd = lax.rem(col, 2)
    place = jnp.where(odd == 0, col // 2, cols - 1 - col // 2)

    def at(place):
        place = lax.rem(place + cols, cols)
        return jnp.where(place < half, 2 * place, 2 * (cols - 1 - place) + 1)

    after, before = at(place + 1), at(place - 1)
    barrier = pltpu.get_barrier_semaphore()
    for step in range(1, rows):
        pl.semaphore_signal(barrier, inc=1, device_id=(lax.rem(row + step, rows), col),
                            device_id_type=MESH_ID)
    for peer in (after, before):
        pl.semaphore_signal(barrier, inc=1, device_id=(row, peer), device_id_type=MESH_ID)
    pl.semaphore_wait(barrier, rows + 1)

    leads = ((0, 0), (1, 0), (1, 1))

    def lead_copy(index, step):
        return pltpu.make_async_remote_copy(
            src_ref=m_ref.at[0, :, 0], dst_ref=l_ref.at[index],
            send_sem=lead_send.at[index, step - 1], recv_sem=lead_recv.at[index],
            device_id=(lax.rem(row + step, rows), col), device_id_type=MESH_ID)

    def lead_own(index):
        return pltpu.make_async_copy(m_ref.at[0, :, 0], l_ref.at[index], own_sem.at[index])

    for index, (lead_row, lead_col) in enumerate(leads):
        @pl.when((row == lead_row) & (col == lead_col))
        def _():
            for step in range(1, rows):
                lead_copy(index, step).start()
            lead_own(index).start()

    def wide_copy(which, step):
        return pltpu.make_async_remote_copy(
            src_ref=m_ref.at[0], dst_ref=c_ref.at[which],
            send_sem=wide_send.at[which, step - 1], recv_sem=wide_recv.at[which],
            device_id=(lax.rem(row + step, rows), col), device_id_type=MESH_ID)

    def wide_own(which):
        return pltpu.make_async_copy(m_ref.at[0], c_ref.at[which], own_sem.at[3 + which])

    def column_own(which):
        return pltpu.make_async_copy(m_ref.at[:, :, 0], r_ref.at[which], own_sem.at[5 + which])

    for which in range(2):
        @pl.when(row == which)
        def _():
            for step in range(1, rows):
                wide_copy(which, step).start()
            wide_own(which).start()

        @pl.when(col == which)
        def _():
            column_own(which).start()

    for index, (lead_row, lead_col) in enumerate(leads):
        @pl.when((row != lead_row) & (col == lead_col))
        def _():
            lead_copy(index, 1).wait_recv()

        @pl.when((row == lead_row) & (col == lead_col))
        def _():
            lead_own(index).wait()

    streams = ((0, 1, 0), (0, -1, 1), (1, 1, 2), (1, -1, None))
    share = depth // 2

    def ring_copy(stream, chunk, first):
        source, way, lead = streams[stream]
        to = after if way == 1 else before
        if chunk == 0:
            src = dst = l_ref.at[lead]
        else:
            index = chunk - 1 + (share if way == -1 else 0)
            dst = r_ref.at[source, index]
            src = m_ref.at[index, :, 0] if first else dst
        return pltpu.make_async_remote_copy(
            src_ref=src, dst_ref=dst, send_sem=ring_send.at[stream, chunk],
            recv_sem=ring_recv.at[stream, chunk], device_id=(row, to),
            device_id_type=MESH_ID)

    starts = (0, cols - 1)
    away = [lax.rem(way * (place - starts[source]) + cols, cols)
            for source, way, _ in streams]
    for chunk in range(share + 1):
        for stream in range(len(streams)):
            if chunk == 0 and streams[stream][2] is None:
                continue

            @pl.when(away[stream] == 0)
            def _():
                ring_copy(stream, chunk, True).start()

            @pl.when(away[stream] > 0)
            def _():
                ring_copy(stream, chunk, False).wait_recv()

            @pl.when((away[stream] > 0) & (away[stream] < cols - 1))
            def _():
                ring_copy(stream, chunk, False).start()

    for chunk in range(share + 1):
        for stream in range(len(streams)):
            if chunk == 0 and streams[stream][2] is None:
                continue

            @pl.when(away[stream] < cols - 1)
            def _():
                ring_copy(stream, chunk, False).wait_send()

    for index, (lead_row, lead_col) in enumerate(leads):
        @pl.when((row == lead_row) & (col == lead_col))
        def _():
            for step in range(1, rows):
                lead_copy(index, step).wait_send()

    for which in range(2):
        @pl.when(row == which)
        def _():
            for step in range(1, rows):
                wide_copy(which, step).wait_send()
            wide_own(which).wait()

        @pl.when(row != which)
        def _():
            wide_copy(which, 1).wait_recv()

        @pl.when(col == which)
        def _():
            column_own(which).wait()


def split(value):
    high = value.astype(jnp.bfloat16)
    return high, (value - high.astype(jnp.float32)).astype(jnp.bfloat16)


def mul(a, b):
    return jnp.dot(a, b, precision=EXACT, preferred_element_type=jnp.float32)


def mul_t(a, b):
    return lax.dot_general(a, b, (((1,), (1,)), ((), ())), precision=EXACT,
                           preferred_element_type=jnp.float32)


def update(width, edge, r_ref, c_ref, f_ref, m_ref, o_ref, high_ref, low_ref):
    index = pl.program_id(0)
    row = lax.axis_index("row")
    col = lax.axis_index("col")
    parts = edge // LANES
    stride = width * parts
    inv0, low10, inv1 = f_ref[0], f_ref[1], f_ref[2]

    def tile(ref, lead, j):
        return jnp.concatenate(
            [ref[lead + (pl.ds(j * parts + h, edge, stride=stride), slice(None))]
             for h in range(parts)], axis=1)

    def put(j, value):
        for h in range(parts):
            o_ref[0, pl.ds(j * parts + h, edge, stride=stride), :] = (
                value[:, h * LANES:(h + 1) * LANES])

    @pl.when(index == 0)
    def _():
        for j in range(width):
            first = mul(inv0, tile(c_ref, (0,), j))
            second = mul(inv1, tile(c_ref, (1,), j) - mul(low10, first))
            here = slice(j * edge, (j + 1) * edge)
            for k, value in enumerate((first, second)):
                high, low = split(value)
                high_ref[k * edge:(k + 1) * edge, here] = high
                low_ref[k * edge:(k + 1) * edge, here] = low

    def column(which):
        return jnp.concatenate(
            [r_ref[which, 0, pl.ds(h, edge, stride=parts), :] for h in range(parts)], axis=1)

    first = mul_t(column(0), inv0)
    second = mul_t(column(1) - mul_t(first, low10), inv1)
    high, low = split(jnp.concatenate([first, second], axis=1))
    for j in range(width):
        here = slice(j * edge, (j + 1) * edge)
        wide_high, wide_low = high_ref[:, here], low_ref[:, here]
        change = jnp.dot(high, wide_low, preferred_element_type=jnp.float32)
        change += jnp.dot(low, wide_high, preferred_element_type=jnp.float32)
        change += jnp.dot(high, wide_high, preferred_element_type=jnp.float32)
        put(j, tile(m_ref, (0,), j) - change)

    @pl.when(col == 0)
    def _():
        put(0, first)

    @pl.when(col == 1)
    def _():
        put(0, second)

    @pl.when((index == 0) & (row < 2))
    def _():
        o_ref[...] = jnp.zeros_like(o_ref)

        @pl.when((row == 0) & (col == 0))
        def _():
            put(0, f_ref[3])

        @pl.when((row == 1) & (col == 0))
        def _():
            put(0, low10)

        @pl.when((row == 1) & (col == 1))
        def _():
            put(0, f_ref[4])


def factors(lead):
    edge = lead.shape[1]
    a00, a10, a11 = lead[0], lead[1], lead[2]
    identity = jnp.eye(edge, dtype=jnp.float32)

    def factor(block):
        low = jnp.linalg.cholesky(block)
        return low, jax.scipy.linalg.solve_triangular(low, identity, lower=True)

    low00, inv0 = factor(a00)
    low10 = mul_t(a10, inv0)
    low11, inv1 = factor(a11 - mul_t(low10, low10))
    return jnp.stack([inv0, low10, inv1, low00, low11])


def local(rows, cols, matrix):
    depth, _, edge, width, _, _ = matrix.shape
    parts = edge // LANES
    any_spec = pl.BlockSpec(memory_space=pl.ANY)
    vmem_spec = pl.BlockSpec(memory_space=pltpu.VMEM)
    dma = pltpu.SemaphoreType.DMA
    share = depth // 2
    f32 = jnp.float32
    panel, wide, lead = pl.pallas_call(
        functools.partial(exchange, rows, cols, depth),
        out_shape=(
            jax.ShapeDtypeStruct((2, depth, edge, parts, LANES), f32),
            jax.ShapeDtypeStruct((2, edge, width, parts, LANES), f32),
            jax.ShapeDtypeStruct((3, edge, parts, LANES), f32),
        ),
        in_specs=[any_spec],
        out_specs=(vmem_spec, vmem_spec, vmem_spec),
        scratch_shapes=[
            dma((4, share + 1)), dma((4, share + 1)), dma((3, rows - 1)), dma((3,)),
            dma((2, rows - 1)), dma((2,)), dma((7,)),
        ],
        compiler_params=pltpu.CompilerParams(collective_id=0, has_side_effects=True),
        name="exchange",
    )(matrix.reshape(depth, edge, width, parts, LANES))
    found = factors(lead.reshape(3, edge, edge))
    lines = edge * width * parts
    result = pl.pallas_call(
        functools.partial(update, width, edge),
        grid=(depth,),
        out_shape=jax.ShapeDtypeStruct((depth, lines, LANES), f32),
        in_specs=[
            pl.BlockSpec((2, 1, edge * parts, LANES), lambda i: (0, i, 0, 0)),
            vmem_spec,
            vmem_spec,
            pl.BlockSpec((1, lines, LANES), lambda i: (i, 0, 0)),
        ],
        out_specs=pl.BlockSpec((1, lines, LANES), lambda i: (i, 0, 0)),
        scratch_shapes=[pltpu.VMEM((2 * edge, width * edge), jnp.bfloat16)] * 2,
        compiler_params=pltpu.CompilerParams(vmem_limit_bytes=48 * 1024 * 1024),
        name="update",
    )(panel.reshape(2, depth, edge * parts, LANES), wide.reshape(2, lines, LANES), found,
      matrix.reshape(depth, lines, LANES))
    return result.reshape(matrix.shape)


def solution(mesh):
    spec = P(None, "row", None, None, "col", None)
    body = functools.partial(local, mesh.shape["row"], mesh.shape["col"])
    return jax.shard_map(body, mesh=mesh, in_specs=(spec,), out_specs=spec, check_vma=False)
```

time: 998 us -> 1370 us (1.37)
  Pallas kernels: 0 us -> 1230 us
  waiting for transfers between devices: 496 us -> 0 us
  local copies, waits for them, and re-layouts: 205 us -> 12.1 us
  matrix products: 101 us -> 3.71 us
  other arithmetic: 163 us -> 109 us
  between operations: 16.8 us -> 3.07 us
    pallas_call x0 -> x2, Pallas kernels: none -> 1230 us  [the longest x1 1150 us: local(): pl.pallas_call(functools.partial(exchange, rows, cols, depth), out_shape=...]
    psum x6 -> x0, waiting for transfers between devices: 496 us -> none  [broadcast(): return lax.psum(kept, axis)]
    unnamed x10 -> x3, local copies, waits for them, and re-layouts: 102 us -> 2.2 us
    dot_general x5 -> x2, matrix products: 98 us -> 1.02 us  [mul_t(): lax.dot_general(a, b, (((1,), (1,)), ((), ())), precision=EXACT, preferre...]
    reshape x1 -> x0, local copies, waits for them, and re-layouts: 78.2 us -> none  [local(): return blocks.reshape(matrix.shape)]
    reshape x1 -> x0, other arithmetic: 22.9 us -> none  [local(): return blocks.reshape(matrix.shape)]
    select_n x7 -> x0, other arithmetic: 22.4 us -> none  [the longest x1 13.3 us: finish(): return jnp.where(zero_row, jnp.zeros_like(blocks), blocks)]
    another operation x18 -> x19, other arithmetic: 108 us -> 108 us  [the longest x13 68.7 us: factor(): low = jnp.linalg.cholesky(block)]
  transfers between devices with their start and end apart: 6 -> 0, of which waited for: 6 -> 0; matrix products, arithmetic and copies ran while one was open for 6% -> 0% of each run, Pallas kernels for 0% -> 0%
where the time goes in v1:
time: 1370 us
  Pallas kernels  1230 us (90%)
  other arithmetic  109 us (8%)
    pallas_call x1, Pallas kernels, local(): pl.pallas_call(functools.partial(exchange, rows, cols, depth), out_shape=...  1150 us
    pallas_call x1, Pallas kernels, local(): pl.pallas_call(functools.partial(update, width, edge), grid=(depth,), out...  76 us
    another operation x13, other arithmetic, factor(): low = jnp.linalg.cholesky(block)  68.7 us
    another operation x5, other arithmetic, factor(): return (low, jax.scipy.linalg.solve_triangular(low, identity, lower=True))  39.7 us

profile of v1, /device:TPU:4, one launch (start us, length us, event | category | flops | bytes accessed | tf_op | source)
XLA Modules:
  0.0 1367.0 jit_solution(9505143060824680893)
XLA Ops:
  0.1 1152.9 %exchange.1 = (f32[2,16,256,2,128]{4,3,2,1,0:T(2,128)}, f32[2,256,8,2,128]{4,3,2,1,0:T(2,128)}, f32[3,256,2,128]{3,2,1,0:T(2,128)}) custom-call(f32[16,256,8,2,128]{4,3,2,1,0:T(2,128)} %bitcast.92), custom_call_target="tpu_custom_call" | custom-call | tf_op jit(solution)/shard_map/exchange/pallas_call | solution.py:260
  1153.1 1.2 fusion.27
  1154.7 11.7 cholesky.130
  1166.5 9.8 custom-call.13
  1176.8 11.7 cholesky.147
  1188.5 0.7 compare_reduce_fusion.2
  1190.6 4.0 while.4
  1190.6 0.6 fusion.40
  1191.2 1.4 bitcast_dynamic-update-slice_fusion.8
  1192.6 0.6 fusion.40
  1193.2 1.4 bitcast_dynamic-update-slice_fusion.8
  1194.6 19.9 %custom-call.14 = f32[2,128,128]{1,2,0:T(8,128)S(1)} custom-call(f32[2,128,128]{2,1,0:T(8,128)S(1)} %get-tuple-element.27), custom_call_target="InvertDiagBlocksLowerTriangular" | custom-call | tf_op jit(solution)/shard_map/jit(_solve_triangular)/triangular_solve | solution.py:244
  1216.8 11.7 cholesky.164
  1228.6 0.7 compare_reduce_fusion.1
  1229.2 9.8 custom-call.15
  1239.6 11.7 cholesky.181
  1251.3 0.7 compare_reduce_fusion
  1253.4 14.5 %while.5 = (s32[]{:T(128)}, f32[256,256]{1,0:T(8,128)S(1)}, s32[2,2]{1,0:T(2,128)S(1)}, f32[2,128,128]{2,1,0:T(8,128)S(1)}, s32[]{:T(128)}) while((s32[]{:T(128)}, f32[256,256]{1,0:T(8,128)S(1)}, s32[2,2]{1,0:T(2,128)S(1)}, f32[2,128,128]{2,1,0:T(8,128)S(1)}, s32[]{:T(128)}) %tuple.51), condition=%wide.while_cond.clone, body=%wide.while_body.clone.sunk | while | flops 2 | bytes 131189 | solution.py:244
  1263.8 0.6 fusion.41
  1264.5 1.4 bitcast_dynamic-update-slice_fusion.9
  1266.5 1.4 bitcast_dynamic-update-slice_fusion.9
  1267.9 19.7 %custom-call.16 = f32[2,128,128]{1,2,0:T(8,128)S(1)} custom-call(f32[2,128,128]{2,1,0:T(8,128)S(1)} %get-tuple-element.28), custom_call_target="InvertDiagBlocksLowerTriangular" | custom-call | tf_op jit(solution)/shard_map/jit(_solve_triangular)/triangular_solve | solution.py:244
  1288.6 2.2 copy-done
  1290.8 76.0 %update.1 = f32[16,4096,128]{2,1,0:T(8,128)} custom-call(f32[2,16,512,128]{3,2,1,0:T(8,128)} %bitcast.94, f32[2,4096,128]{2,1,0:T(8,128)S(1)} %bitcast.91, f32[5,256,256]{2,1,0:T(8,128)S(1)} %bitcast_dynamic-update-slice_fusion.3.f_ref, f32[16,4096,128]{2,1,0:T(8,128)} %bitcast.93), custom_call_target="tpu_custom_call" | custom-call | tf_op jit(solution)/shard_map/update/pallas_call | solution.py:278
  (45 shorter events, 5.6 us)
Async XLA Ops:
  1288.6 2.2 copy-start

commit v2 on v1

--- a/solution.py
+++ b/solution.py
@@ -8,11 +8,12 @@
 from jax.sharding import PartitionSpec as P
 
 LANES = 128
+PIECES = 4
 MESH_ID = pl.DeviceIdType.MESH
 EXACT = lax.Precision.HIGHEST
 
 
-def exchange(rows, cols, depth, m_ref, r_ref, c_ref, l_ref, ring_send, ring_recv,
+def exchange(rows, cols, depth, p_ref, m_ref, r_ref, c_ref, l_ref, ring_send, ring_recv,
              lead_send, lead_recv, wide_send, wide_recv, own_sem):
     row = lax.axis_index("row")
     col = lax.axis_index("col")
@@ -37,12 +38,12 @@
 
     def lead_copy(index, step):
         return pltpu.make_async_remote_copy(
-            src_ref=m_ref.at[0, :, 0], dst_ref=l_ref.at[index],
+            src_ref=p_ref.at[pl.ds(0, PIECES)], dst_ref=l_ref.at[index],
             send_sem=lead_send.at[index, step - 1], recv_sem=lead_recv.at[index],
             device_id=(lax.rem(row + step, rows), col), device_id_type=MESH_ID)
 
     def lead_own(index):
-        return pltpu.make_async_copy(m_ref.at[0, :, 0], l_ref.at[index], own_sem.at[index])
+        return pltpu.make_async_copy(p_ref.at[pl.ds(0, PIECES)], l_ref.at[index], own_sem.at[index])
 
     for index, (lead_row, lead_col) in enumerate(leads):
         @pl.when((row == lead_row) & (col == lead_col))
@@ -61,7 +62,7 @@
         return pltpu.make_async_copy(m_ref.at[0], c_ref.at[which], own_sem.at[3 + which])
 
     def column_own(which):
-        return pltpu.make_async_copy(m_ref.at[:, :, 0], r_ref.at[which], own_sem.at[5 + which])
+        return pltpu.make_async_copy(p_ref, r_ref.at[which], own_sem.at[5 + which])
 
     for which in range(2):
         @pl.when(row == which)
@@ -84,50 +85,63 @@
             lead_own(index).wait()
 
     streams = ((0, 1, 0), (0, -1, 1), (1, 1, 2), (1, -1, None))
-    share = depth // 2
-
-    def ring_copy(stream, chunk, first):
-        source, way, lead = streams[stream]
-        to = after if way == 1 else before
-        if chunk == 0:
-            src = dst = l_ref.at[lead]
+    share = depth // 2 * PIECES
+    total = share + PIECES
+
+    def ring_copy(stream, piece, lead, first):
+        source, way, block = streams[stream]
+        if lead:
+            src = dst = l_ref.at[block, piece]
         else:
-            index = chunk - 1 + (share if way == -1 else 0)
+            index = piece - PIECES + (share if way == -1 else 0)
             dst = r_ref.at[source, index]
-            src = m_ref.at[index, :, 0] if first else dst
+            src = p_ref.at[index] if first else dst
         return pltpu.make_async_remote_copy(
-            src_ref=src, dst_ref=dst, send_sem=ring_send.at[stream, chunk],
-            recv_sem=ring_recv.at[stream, chunk], device_id=(row, to),
-            device_id_type=MESH_ID)
+            src_ref=src, dst_ref=dst, send_sem=ring_send.at[stream, piece],
+            recv_sem=ring_recv.at[stream, piece],
+            device_id=(row, after if way == 1 else before), device_id_type=MESH_ID)
 
     starts = (0, cols - 1)
     away = [lax.rem(way * (place - starts[source]) + cols, cols)
             for source, way, _ in streams]
-    for chunk in range(share + 1):
+
+    def serve(stream, piece, lead):
+        @pl.when(away[stream] == 0)
+        def _():
+            ring_copy(stream, piece, lead, True).start()
+
+        @pl.when(away[stream] > 0)
+        def _():
+            ring_copy(stream, piece, lead, False).wait_recv()
+
+        @pl.when((away[stream] > 0) & (away[stream] < cols - 1))
+        def _():
+            ring_copy(stream, piece, lead, False).start()
+
+    @pl.loop(0, total + cols - 1)
+    def _(moment):
         for stream in range(len(streams)):
-            if chunk == 0 and streams[stream][2] is None:
-                continue
-
-            @pl.when(away[stream] == 0)
+            piece = moment - away[stream]
+            if streams[stream][2] is not None:
+                @pl.when((piece >= 0) & (piece < PIECES))
+                def _():
+                    serve(stream, piece, True)
+
+            @pl.when((piece >= PIECES) & (piece < total))
             def _():
-                ring_copy(stream, chunk, True).start()
-
-            @pl.when(away[stream] > 0)
-            def _():
-                ring_copy(stream, chunk, False).wait_recv()
-
-            @pl.when((away[stream] > 0) & (away[stream] < cols - 1))
-            def _():
-                ring_copy(stream, chunk, False).start()
-
-    for chunk in range(share + 1):
-        for stream in range(len(streams)):
-            if chunk == 0 and streams[stream][2] is None:
-                continue
-
-            @pl.when(away[stream] < cols - 1)
-            def _():
-                ring_copy(stream, chunk, False).wait_send()
+                serve(stream, piece, False)
+
+    for stream in range(len(streams)):
+        @pl.when(away[stream] < cols - 1)
+        def _():
+            if streams[stream][2] is not None:
+                @pl.loop(0, PIECES)
+                def _(piece):
+                    ring_copy(stream, piece, True, False).wait_send()
+
+            @pl.loop(PIECES, total)
+            def _(piece):
+                ring_copy(stream, piece, False, False).wait_send()
 
     for index, (lead_row, lead_col) in enumerate(leads):
         @pl.when((row == lead_row) & (col == lead_col))
@@ -165,7 +179,7 @@
                            preferred_element_type=jnp.float32)
 
 
-def update(width, edge, r_ref, c_ref, f_ref, m_ref, o_ref, high_ref, low_ref):
+def update(width, edge, r_ref, c_ref, f_ref, m_ref, o_ref, stack_ref):
     index = pl.program_id(0)
     row = lax.axis_index("row")
     col = lax.axis_index("col")
@@ -191,22 +205,16 @@
             here = slice(j * edge, (j + 1) * edge)
             for k, value in enumerate((first, second)):
                 high, low = split(value)
-                high_ref[k * edge:(k + 1) * edge, here] = high
-                low_ref[k * edge:(k + 1) * edge, here] = low
-
-    def column(which):
-        return jnp.concatenate(
-            [r_ref[which, 0, pl.ds(h, edge, stride=parts), :] for h in range(parts)], axis=1)
-
-    first = mul_t(column(0), inv0)
-    second = mul_t(column(1) - mul_t(first, low10), inv1)
+                for slot, half in enumerate((low, high, high)):
+                    stack_ref[(2 * slot + k) * edge:(2 * slot + k + 1) * edge, here] = half
+
+    first = mul_t(r_ref[0, 0], inv0)
+    second = mul_t(r_ref[1, 0] - mul_t(first, low10), inv1)
     high, low = split(jnp.concatenate([first, second], axis=1))
+    stack = jnp.concatenate([high, high, low], axis=1)
     for j in range(width):
         here = slice(j * edge, (j + 1) * edge)
-        wide_high, wide_low = high_ref[:, here], low_ref[:, here]
-        change = jnp.dot(high, wide_low, preferred_element_type=jnp.float32)
-        change += jnp.dot(low, wide_high, preferred_element_type=jnp.float32)
-        change += jnp.dot(high, wide_high, preferred_element_type=jnp.float32)
+        change = jnp.dot(stack, stack_ref[:, here], preferred_element_type=jnp.float32)
         put(j, tile(m_ref, (0,), j) - change)
 
     @pl.when(col == 0)
@@ -234,18 +242,26 @@
             put(0, f_ref[4])
 
 
+def factor(block):
+    half = block.shape[0] // 2
+    identity = jnp.eye(half, dtype=jnp.float32)
+    zero = jnp.zeros_like(identity)
+
+    def one(part):
+        low = jnp.linalg.cholesky(part)
+        return low, jax.scipy.linalg.solve_triangular(low, identity, lower=True)
+
+    top, inv_top = one(block[:half, :half])
+    side = mul_t(block[half:, :half], inv_top)
+    end, inv_end = one(block[half:, half:] - mul_t(side, side))
+    corner = -mul(inv_end, mul(side, inv_top))
+    return jnp.block([[top, zero], [side, end]]), jnp.block([[inv_top, zero], [corner, inv_end]])
+
+
 def factors(lead):
-    edge = lead.shape[1]
-    a00, a10, a11 = lead[0], lead[1], lead[2]
-    identity = jnp.eye(edge, dtype=jnp.float32)
-
-    def factor(block):
-        low = jnp.linalg.cholesky(block)
-        return low, jax.scipy.linalg.solve_triangular(low, identity, lower=True)
-
-    low00, inv0 = factor(a00)
-    low10 = mul_t(a10, inv0)
-    low11, inv1 = factor(a11 - mul_t(low10, low10))
+    low00, inv0 = factor(lead[0])
+    low10 = mul_t(lead[1], inv0)
+    low11, inv1 = factor(lead[2] - mul_t(low10, low10))
     return jnp.stack([inv0, low10, inv1, low00, low11])
 
 
@@ -255,41 +271,41 @@
     any_spec = pl.BlockSpec(memory_space=pl.ANY)
     vmem_spec = pl.BlockSpec(memory_space=pltpu.VMEM)
     dma = pltpu.SemaphoreType.DMA
-    share = depth // 2
+    total = (depth // 2 + 1) * PIECES
+    lines = edge * width * parts
     f32 = jnp.float32
     panel, wide, lead = pl.pallas_call(
         functools.partial(exchange, rows, cols, depth),
         out_shape=(
-            jax.ShapeDtypeStruct((2, depth, edge, parts, LANES), f32),
-            jax.ShapeDtypeStruct((2, edge, width, parts, LANES), f32),
-            jax.ShapeDtypeStruct((3, edge, parts, LANES), f32),
+            jax.ShapeDtypeStruct((2, depth * PIECES, edge // PIECES, edge), f32),
+            jax.ShapeDtypeStruct((2, lines, LANES), f32),
+            jax.ShapeDtypeStruct((3, PIECES, edge // PIECES, edge), f32),
         ),
-        in_specs=[any_spec],
+        in_specs=[any_spec, any_spec],
         out_specs=(vmem_spec, vmem_spec, vmem_spec),
         scratch_shapes=[
-            dma((4, share + 1)), dma((4, share + 1)), dma((3, rows - 1)), dma((3,)),
+            dma((4, total)), dma((4, total)), dma((3, rows - 1)), dma((3,)),
             dma((2, rows - 1)), dma((2,)), dma((7,)),
         ],
         compiler_params=pltpu.CompilerParams(collective_id=0, has_side_effects=True),
         name="exchange",
-    )(matrix.reshape(depth, edge, width, parts, LANES))
+    )(matrix[:, 0, :, 0, 0, :].reshape(depth * PIECES, edge // PIECES, edge), matrix.reshape(depth, lines, LANES))
     found = factors(lead.reshape(3, edge, edge))
-    lines = edge * width * parts
     result = pl.pallas_call(
         functools.partial(update, width, edge),
         grid=(depth,),
         out_shape=jax.ShapeDtypeStruct((depth, lines, LANES), f32),
         in_specs=[
-            pl.BlockSpec((2, 1, edge * parts, LANES), lambda i: (0, i, 0, 0)),
+            pl.BlockSpec((2, 1, edge, edge), lambda i: (0, i, 0, 0)),
             vmem_spec,
             vmem_spec,
             pl.BlockSpec((1, lines, LANES), lambda i: (i, 0, 0)),
         ],
         out_specs=pl.BlockSpec((1, lines, LANES), lambda i: (i, 0, 0)),
-        scratch_shapes=[pltpu.VMEM((2 * edge, width * edge), jnp.bfloat16)] * 2,
+        scratch_shapes=[pltpu.VMEM((6 * edge, width * edge), jnp.bfloat16)],
         compiler_params=pltpu.CompilerParams(vmem_limit_bytes=48 * 1024 * 1024),
         name="update",
-    )(panel.reshape(2, depth, edge * parts, LANES), wide.reshape(2, lines, LANES), found,
+    )(panel.reshape(2, depth, edge, edge), wide, found,
       matrix.reshape(depth, lines, LANES))
     return result.reshape(matrix.shape)
 

time: 1370 us -> 352 us (0.26)
  Pallas kernels: 1230 us -> 240 us
  other arithmetic: 109 us -> 92.1 us
    pallas_call x1, Pallas kernels: 1150 us -> 164 us  [local(): pl.pallas_call(functools.partial(exchange, rows, cols, depth), out_shape=...]
    another operation x18 -> x20, other arithmetic: 108 us -> 92 us  [the longest x12 49.7 us: one(): low = jnp.linalg.cholesky(part)]
where the time goes in v2:
time: 352 us; the launch traced here: 348 us
  Pallas kernels  240 us (68%)
  other arithmetic  92.1 us (26%)
  local copies, waits for them, and re-layouts  11.8 us (3%)
  matrix products  4.12 us (1%)
    pallas_call x1, Pallas kernels, local(): pl.pallas_call(functools.partial(exchange, rows, cols, depth), out_shape=...  164 us
    pallas_call x1, Pallas kernels, local(): pl.pallas_call(functools.partial(update, width, edge), grid=(depth,), out...  75.9 us
    another operation x12, other arithmetic, one(): low = jnp.linalg.cholesky(part)  49.7 us
    another operation x8, other arithmetic, one(): return (low, jax.scipy.linalg.solve_triangular(low, identity, lower=True))  42.2 us

profile of v2, /device:TPU:4, one launch (start us, length us, event | category | flops | bytes accessed | tf_op | source)
XLA Modules:
  0.0 348.4 jit_solution(16201042437739198663)
XLA Ops:
  0.0 5.1 %slice.41 = f32[16,1,256,1,1,256]{5,4,3,2,1,0:T(1,128)S(1)} slice(f32[16,1,256,8,1,256]{5,4,3,2,1,0:T(1,128)} %param.4), slice={[0:16], [0:1], [0:256], [0:1], [0:1], [0:256]} | slice | bytes 8388608 | tf_op jit(solution)/shard_map/slice | solution.py:292
  5.1 2.4 copy.40
  7.5 164.0 %exchange.1 = (f32[2,64,64,256]{3,2,1,0:T(8,128)}, f32[2,4096,128]{2,1,0:T(8,128)}, f32[3,4,64,256]{3,2,1,0:T(8,128)}) custom-call(f32[64,64,256]{2,1,0:T(8,128)} %bitcast.78, f32[16,4096,128]{2,1,0:T(8,128)} %bitcast.76), custom_call_target="tpu_custom_call" | custom-call | tf_op jit(solution)/shard_map/exchange/pallas_call | solution.py:277
  171.5 1.2 fusion.34
  172.9 11.7 %cholesky.74 = f32[128,128]{1,0:T(8,128)S(1)} custom-call(f32[128,128]{1,0:T(8,128)S(1)} %get-tuple-element.24), custom_call_target="Cholesky" | custom-call | tf_op jit(solution)/shard_map/jit(cholesky)/cholesky | solution.py:251
  184.7 0.6 compare_reduce_fusion.3
  185.3 0.7 select_bitcast_fusion.3
  186.0 9.8 %custom-call.8 = f32[1,128,128]{1,2,0:T(8,128)S(1)} custom-call(f32[1,128,128]{2,1,0:T(8,128)S(1)} %get-tuple-element.19), custom_call_target="InvertDiagBlocksLowerTriangular" | custom-call | tf_op jit(solution)/shard_map/jit(_solve_triangular)/triangular_solve | solution.py:252
  197.3 11.7 %cholesky.85 = f32[128,128]{1,0:T(8,128)S(1)} custom-call(f32[128,128]{1,0:T(8,128)S(1)} %fusion.26), custom_call_target="Cholesky" | custom-call | tf_op jit(solution)/shard_map/jit(cholesky)/cholesky | solution.py:251
  209.0 0.6 compare_reduce_fusion.2
  209.7 0.7 select_bitcast_fusion.2
  210.3 10.2 %custom-call.9 = f32[1,128,128]{1,2,0:T(8,128)S(1)} custom-call(f32[1,128,128]{2,1,0:T(8,128)S(1)} %get-tuple-element.17), custom_call_target="InvertDiagBlocksLowerTriangular" | custom-call | tf_op jit(solution)/shard_map/jit(_solve_triangular)/triangular_solve | solution.py:252
  221.2 0.4 bitcast_dynamic-update-slice_fusion
  221.6 0.4 convolution_subtract_fusion
  222.2 11.7 %cholesky.96 = f32[128,128]{1,0:T(8,128)S(1)} custom-call(f32[128,128]{1,0:T(8,128)S(1)} %fusion.24), custom_call_target="Cholesky" | custom-call | tf_op jit(solution)/shard_map/jit(cholesky)/cholesky | solution.py:251
  233.9 0.6 compare_reduce_fusion.1
  234.6 0.7 select_bitcast_fusion.1
  235.2 9.8 %custom-call.10 = f32[1,128,128]{1,2,0:T(8,128)S(1)} custom-call(f32[1,128,128]{2,1,0:T(8,128)S(1)} %get-tuple-element.15), custom_call_target="InvertDiagBlocksLowerTriangular" | custom-call | tf_op jit(solution)/shard_map/jit(_solve_triangular)/triangular_solve | solution.py:252
  246.0 11.9 %cholesky.107 = f32[128,128]{1,0:T(8,128)S(1)} custom-call(f32[128,128]{1,0:T(8,128)S(1)} %fusion.22), custom_call_target="Cholesky" | custom-call | tf_op jit(solution)/shard_map/jit(cholesky)/cholesky | solution.py:251
  257.9 0.6 compare_reduce_fusion
  258.5 0.7 select_bitcast_fusion
  259.2 9.8 %custom-call.11 = f32[1,128,128]{1,2,0:T(8,128)S(1)} custom-call(f32[1,128,128]{2,1,0:T(8,128)S(1)} %get-tuple-element.13), custom_call_target="InvertDiagBlocksLowerTriangular" | custom-call | tf_op jit(solution)/shard_map/jit(_solve_triangular)/triangular_solve | solution.py:252
  270.1 2.2 copy-done
  272.3 75.9 %update.1 = f32[16,4096,128]{2,1,0:T(8,128)} custom-call(f32[2,16,256,256]{3,2,1,0:T(8,128)} %bitcast.79, f32[2,4096,128]{2,1,0:T(8,128)S(1)} %copy-done, f32[5,256,256]{2,1,0:T(8,128)S(1)} %fusion.1.f_ref, f32[16,4096,128]{2,1,0:T(8,128)} %bitcast.77), custom_call_target="tpu_custom_call" | custom-call | tf_op jit(solution)/shard_map/update/pallas_call | solution.py:294
  (37 shorter events, 4.5 us)
Async XLA Ops:
  270.1 2.2 copy-start

commit v3 on v2

--- a/solution.py
+++ b/solution.py
@@ -61,8 +61,8 @@
     def wide_own(which):
         return pltpu.make_async_copy(m_ref.at[0], c_ref.at[which], own_sem.at[3 + which])
 
-    def column_own(which):
-        return pltpu.make_async_copy(p_ref, r_ref.at[which], own_sem.at[5 + which])
+    def column_own():
+        return pltpu.make_async_copy(p_ref, r_ref, own_sem.at[5])
 
     for which in range(2):
         @pl.when(row == which)
@@ -71,9 +71,9 @@
                 wide_copy(which, step).start()
             wide_own(which).start()
 
-        @pl.when(col == which)
-        def _():
-            column_own(which).start()
+    @pl.when(col == 0)
+    def _():
+        column_own().start()
 
     for index, (lead_row, lead_col) in enumerate(leads):
         @pl.when((row != lead_row) & (col == lead_col))
@@ -84,7 +84,7 @@
         def _():
             lead_own(index).wait()
 
-    streams = ((0, 1, 0), (0, -1, 1), (1, 1, 2), (1, -1, None))
+    streams = ((0, 1, 0), (0, -1, 1), (1, 1, 2))
     share = depth // 2 * PIECES
     total = share + PIECES
 
@@ -94,7 +94,7 @@
             src = dst = l_ref.at[block, piece]
         else:
             index = piece - PIECES + (share if way == -1 else 0)
-            dst = r_ref.at[source, index]
+            dst = r_ref.at[index]
             src = p_ref.at[index] if first else dst
         return pltpu.make_async_remote_copy(
             src_ref=src, dst_ref=dst, send_sem=ring_send.at[stream, piece],
@@ -122,26 +122,27 @@
     def _(moment):
         for stream in range(len(streams)):
             piece = moment - away[stream]
-            if streams[stream][2] is not None:
-                @pl.when((piece >= 0) & (piece < PIECES))
+
+            @pl.when((piece >= 0) & (piece < PIECES))
+            def _():
+                serve(stream, piece, True)
+
+            if streams[stream][0] == 0:
+                @pl.when((piece >= PIECES) & (piece < total))
                 def _():
-                    serve(stream, piece, True)
-
-            @pl.when((piece >= PIECES) & (piece < total))
-            def _():
-                serve(stream, piece, False)
+                    serve(stream, piece, False)
 
     for stream in range(len(streams)):
         @pl.when(away[stream] < cols - 1)
         def _():
-            if streams[stream][2] is not None:
-                @pl.loop(0, PIECES)
+            @pl.loop(0, PIECES)
+            def _(piece):
+                ring_copy(stream, piece, True, False).wait_send()
+
+            if streams[stream][0] == 0:
+                @pl.loop(PIECES, total)
                 def _(piece):
-                    ring_copy(stream, piece, True, False).wait_send()
-
-            @pl.loop(PIECES, total)
-            def _(piece):
-                ring_copy(stream, piece, False, False).wait_send()
+                    ring_copy(stream, piece, False, False).wait_send()
 
     for index, (lead_row, lead_col) in enumerate(leads):
         @pl.when((row == lead_row) & (col == lead_col))
@@ -160,9 +161,9 @@
         def _():
             wide_copy(which, 1).wait_recv()
 
-        @pl.when(col == which)
-        def _():
-            column_own(which).wait()
+    @pl.when(col == 0)
+    def _():
+        column_own().wait()
 
 
 def split(value):
@@ -179,7 +180,17 @@
                            preferred_element_type=jnp.float32)
 
 
-def update(width, edge, r_ref, c_ref, f_ref, m_ref, o_ref, stack_ref):
+def short(a, b, dim):
+    (a_high, a_low), (b_high, b_low) = split(a), split(b)
+
+    def dot(x, y):
+        return lax.dot_general(x, y, (((1,), (dim,)), ((), ())),
+                               preferred_element_type=jnp.float32)
+
+    return dot(a_high, b_low) + dot(a_low, b_high) + dot(a_high, b_high)
+
+
+def update(width, edge, r_ref, s_ref, c_ref, f_ref, m_ref, o_ref, stack_ref):
     index = pl.program_id(0)
     row = lax.axis_index("row")
     col = lax.axis_index("col")
@@ -200,16 +211,16 @@
     @pl.when(index == 0)
     def _():
         for j in range(width):
-            first = mul(inv0, tile(c_ref, (0,), j))
-            second = mul(inv1, tile(c_ref, (1,), j) - mul(low10, first))
+            first = short(inv0, tile(c_ref, (0,), j), 0)
+            second = short(inv1, tile(c_ref, (1,), j) - short(low10, first, 0), 0)
             here = slice(j * edge, (j + 1) * edge)
             for k, value in enumerate((first, second)):
                 high, low = split(value)
                 for slot, half in enumerate((low, high, high)):
                     stack_ref[(2 * slot + k) * edge:(2 * slot + k + 1) * edge, here] = half
 
-    first = mul_t(r_ref[0, 0], inv0)
-    second = mul_t(r_ref[1, 0] - mul_t(first, low10), inv1)
+    first = short(r_ref[0], inv0, 1)
+    second = short(s_ref[0] - short(first, low10, 1), inv1, 1)
     high, low = split(jnp.concatenate([first, second], axis=1))
     stack = jnp.concatenate([high, high, low], axis=1)
     for j in range(width):
@@ -274,29 +285,32 @@
     total = (depth // 2 + 1) * PIECES
     lines = edge * width * parts
     f32 = jnp.float32
+    column = matrix[:, 0, :, 0, 0, :]
+    other = lax.psum(jnp.where(lax.axis_index("col") == 1, column, 0), "col")
     panel, wide, lead = pl.pallas_call(
         functools.partial(exchange, rows, cols, depth),
         out_shape=(
-            jax.ShapeDtypeStruct((2, depth * PIECES, edge // PIECES, edge), f32),
+            jax.ShapeDtypeStruct((depth * PIECES, edge // PIECES, edge), f32),
             jax.ShapeDtypeStruct((2, lines, LANES), f32),
             jax.ShapeDtypeStruct((3, PIECES, edge // PIECES, edge), f32),
         ),
         in_specs=[any_spec, any_spec],
         out_specs=(vmem_spec, vmem_spec, vmem_spec),
         scratch_shapes=[
-            dma((4, total)), dma((4, total)), dma((3, rows - 1)), dma((3,)),
-            dma((2, rows - 1)), dma((2,)), dma((7,)),
+            dma((3, total)), dma((3, total)), dma((3, rows - 1)), dma((3,)),
+            dma((2, rows - 1)), dma((2,)), dma((6,)),
         ],
         compiler_params=pltpu.CompilerParams(collective_id=0, has_side_effects=True),
         name="exchange",
-    )(matrix[:, 0, :, 0, 0, :].reshape(depth * PIECES, edge // PIECES, edge), matrix.reshape(depth, lines, LANES))
+    )(column.reshape(depth * PIECES, edge // PIECES, edge), matrix.reshape(depth, lines, LANES))
     found = factors(lead.reshape(3, edge, edge))
     result = pl.pallas_call(
         functools.partial(update, width, edge),
         grid=(depth,),
         out_shape=jax.ShapeDtypeStruct((depth, lines, LANES), f32),
         in_specs=[
-            pl.BlockSpec((2, 1, edge, edge), lambda i: (0, i, 0, 0)),
+            pl.BlockSpec((1, edge, edge), lambda i: (i, 0, 0)),
+            pl.BlockSpec((1, edge, edge), lambda i: (i, 0, 0)),
             vmem_spec,
             vmem_spec,
             pl.BlockSpec((1, lines, LANES), lambda i: (i, 0, 0)),
@@ -305,7 +319,7 @@
         scratch_shapes=[pltpu.VMEM((6 * edge, width * edge), jnp.bfloat16)],
         compiler_params=pltpu.CompilerParams(vmem_limit_bytes=48 * 1024 * 1024),
         name="update",
-    )(panel.reshape(2, depth, edge, edge), wide, found,
+    )(panel.reshape(depth, edge, edge), other, wide, found,
       matrix.reshape(depth, lines, LANES))
     return result.reshape(matrix.shape)
 

time: 352 us -> 413 us (1.17)
  the two profiles are of different devices: /device:TPU:4 before, /device:TPU:6 now
where the time goes in v3:
time: 413 us; the launch traced here: 410 us
  Pallas kernels  280 us (68%)
  other arithmetic  98.7 us (24%)
  between operations  14.2 us (3%)
  local copies, waits for them, and re-layouts  12.1 us (3%)
  matrix products  4.13 us (1%)
    pallas_call x1, Pallas kernels, local(): pl.pallas_call(functools.partial(exchange, rows, cols, depth), out_shape=...  214 us
    pallas_call x1, Pallas kernels, local(): pl.pallas_call(functools.partial(update, width, edge), grid=(depth,), out...  66.5 us
    another operation x12, other arithmetic, one(): low = jnp.linalg.cholesky(part)  49.8 us
    another operation x8, other arithmetic, one(): return (low, jax.scipy.linalg.solve_triangular(low, identity, lower=True))  42.1 us
  transfers between devices with their start and end apart: 1, of which 0 were waited for; matrix products, arithmetic and copies ran while one was open for 24% of the time, Pallas kernels for 52%

profile of v3, /device:TPU:6, one launch (start us, length us, event | category | flops | bytes accessed | tf_op | source)
XLA Modules:
  0.0 409.6 jit_solution(9753362108396411730)
XLA Ops:
  6.5 7.8 %slice.41 = f32[16,1,256,1,1,256]{5,4,3,2,1,0:T(1,128)} slice(f32[16,1,256,8,1,256]{5,4,3,2,1,0:T(1,128)} %param.4), slice={[0:16], [0:1], [0:256], [0:1], [0:1], [0:256]} | slice | bytes 8388608 | tf_op jit(solution)/shard_map/slice | solution.py:288
  14.3 6.7 %select_bitcast_fusion = (f32[16,256,256]{2,1,0:T(8,128)}, f32[16,1,256,1,1,256]{5,2,0,4,3,1:T(8,128)}) fusion(pred[]{:T(512)S(6)} %eq.13, f32[16,1,256,1,1,256]{5,4,3,2,1,0:T(1,128)} %slice.41), kind=kLoop, calls=%fused_computation | loop fusion | flops 1048576 | bytes 12582913 | tf_op jit(solution)/shard_map/jit(_where)/select_n | solution.py:289
  21.1 213.9 %exchange.1 = (f32[64,64,256]{2,1,0:T(8,128)}, f32[2,4096,128]{2,1,0:T(8,128)}, f32[3,4,64,256]{3,2,1,0:T(8,128)}) custom-call(f32[64,64,256]{2,1,0:T(8,128)} %bitcast.81, f32[16,4096,128]{2,1,0:T(8,128)} %bitcast.79), custom_call_target="tpu_custom_call" | custom-call | tf_op jit(solution)/shard_map/exchange/pallas_call | solution.py:290
  235.0 1.2 fusion.34
  236.3 11.7 %cholesky.74 = f32[128,128]{1,0:T(8,128)S(1)} custom-call(f32[128,128]{1,0:T(8,128)S(1)} %get-tuple-element.26), custom_call_target="Cholesky" | custom-call | tf_op jit(solution)/shard_map/jit(cholesky)/cholesky | solution.py:262
  248.0 0.6 compare_reduce_fusion.3
  248.7 0.7 select_bitcast_fusion.4
  249.3 9.8 %custom-call.8 = f32[1,128,128]{1,2,0:T(8,128)S(1)} custom-call(f32[1,128,128]{2,1,0:T(8,128)S(1)} %get-tuple-element.19), custom_call_target="InvertDiagBlocksLowerTriangular" | custom-call | tf_op jit(solution)/shard_map/jit(_solve_triangular)/triangular_solve | solution.py:263
  260.2 11.7 %cholesky.85 = f32[128,128]{1,0:T(8,128)S(1)} custom-call(f32[128,128]{1,0:T(8,128)S(1)} %fusion.26), custom_call_target="Cholesky" | custom-call | tf_op jit(solution)/shard_map/jit(cholesky)/cholesky | solution.py:262
  272.0 0.6 compare_reduce_fusion.2
  272.6 0.7 select_bitcast_fusion.3
  273.3 10.0 %custom-call.9 = f32[1,128,128]{1,2,0:T(8,128)S(1)} custom-call(f32[1,128,128]{2,1,0:T(8,128)S(1)} %get-tuple-element.17), custom_call_target="InvertDiagBlocksLowerTriangular" | custom-call | tf_op jit(solution)/shard_map/jit(_solve_triangular)/triangular_solve | solution.py:263
  284.5 0.4 bitcast_dynamic-update-slice_fusion
  284.9 0.4 convolution_subtract_fusion
  285.5 11.7 %cholesky.96 = f32[128,128]{1,0:T(8,128)S(1)} custom-call(f32[128,128]{1,0:T(8,128)S(1)} %fusion.24), custom_call_target="Cholesky" | custom-call | tf_op jit(solution)/shard_map/jit(cholesky)/cholesky | solution.py:262
  297.2 0.6 compare_reduce_fusion.1
  297.9 0.7 select_bitcast_fusion.2
  298.5 9.8 %custom-call.10 = f32[1,128,128]{1,2,0:T(8,128)S(1)} custom-call(f32[1,128,128]{2,1,0:T(8,128)S(1)} %get-tuple-element.15), custom_call_target="InvertDiagBlocksLowerTriangular" | custom-call | tf_op jit(solution)/shard_map/jit(_solve_triangular)/triangular_solve | solution.py:263
  309.4 12.0 %cholesky.107 = f32[128,128]{1,0:T(8,128)S(1)} custom-call(f32[128,128]{1,0:T(8,128)S(1)} %fusion.22), custom_call_target="Cholesky" | custom-call | tf_op jit(solution)/shard_map/jit(cholesky)/cholesky | solution.py:262
  321.4 0.6 compare_reduce_fusion
  322.0 0.7 select_bitcast_fusion.1
  322.7 9.8 %custom-call.11 = f32[1,128,128]{1,2,0:T(8,128)S(1)} custom-call(f32[1,128,128]{2,1,0:T(8,128)S(1)} %get-tuple-element.13), custom_call_target="InvertDiagBlocksLowerTriangular" | custom-call | tf_op jit(solution)/shard_map/jit(_solve_triangular)/triangular_solve | solution.py:263
  333.6 2.2 copy-done
  335.7 66.5 %update.1 = f32[16,4096,128]{2,1,0:T(8,128)} custom-call(f32[16,256,256]{2,1,0:T(8,128)S(1)} %bitcast.78, f32[16,256,256]{2,1,0:T(8,128)} %all-reduce.6.cloned.1.call-done.s_ref, f32[2,4096,128]{2,1,0:T(8,128)} %get-tuple-element.11.c_ref, f32[5,256,256]{2,1,0:T(8,128)S(1)} %fusion.1.f_ref, f32[16,4096,128]{2,1,0:T(8,128)} %bitcast.80), custom_call_target="tpu_custom_call" | custom-call | tf_op jit(solution)/shard_map/update/pallas_call | solution.py:307
  (40 shorter events, 4.6 us)
Async XLA Ops:
  6.5 327.0 %all-reduce.6.cloned.1.call-start = ((), (), s32[]{:S(2)}) async-start(), calls=%async_computation | async-start | bytes 8388608 | tf_op jit(solution)/shard_map/psum | solution.py:289
  333.5 2.2 copy-start
Sparse Core Ops, SparseCore 0:
  21.2 215.8 all-reduce.5
